TPU v7x, 32 devices: a whole 2x2x4 slice. The times are simulated.
32 devices in a mesh: groups: 2 (over y), wide: 4 (over z), narrow: 2 (over x), sub: 2 (over core).
Axes of the slice: x: 2, y: 2, z: 4, core: 2. Of those that a mesh axis runs over, the one named last changes fastest.
Arguments:
- mode_shapes: bfloat16 [48, 1024, 1024], P(('groups', 'wide'), 'narrow'), parts along dimension 0, may hold values from -0.25 to 0.25
- amplitudes: bfloat16 [2048, 64], P('groups', 'sub'), parts along dimension 0, may hold values from -6 to 6
- self_resistance: float32 [48, 1024], P(('groups', 'wide'), 'narrow'), parts along dimension 0, may hold values from 0.2 to 2
- out_factor: bfloat16 [48, 2, 1024, 256], P(('groups', 'wide'), None, 'narrow'), parts along dimension 0, may hold values from -0.375 to 0.375
- in_factor: bfloat16 [48, 2, 1024, 256], P(('groups', 'wide'), None, 'narrow'), parts along dimension 0, may hold values from -0.1875 to 0.1875
- block_source: int32 [96, 1], P('groups'), parts along dimension 0, may hold values from 0 to 3; in each aligned block of 12 rows (0 to 11, 12 to 23, ...) at most 3 rows name the same one
- block_cluster: int32 [96], P('groups'), parts along dimension 0, may hold values from 0 to 5
- block_rank: int32 [96], P('groups'), parts along dimension 0, may hold values from 64 to 256
Outputs:
- patch_force: bfloat16 [48, 64, 1024], P(('groups', 'wide'), 'sub', 'narrow'), parts along dimension 0
- modal_load: float32 [2048, 64], P(('groups', 'wide', 'narrow'), 'sub'), parts along dimension 0
There are 2 independent parts, one for each index of `groups`. A program takes and returns all parts, laid end to end along the dimension named above; each array names one. Nothing has to cross between parts.
Inputs may be any that keep to these rules, and one draw needn't show every extreme that they name: Among the 12 blocks of one wide index (rows of block_source in aligned runs of that length), at most 3 name the same wide index, and some wide index is named exactly 3 times.
All inputs are finite; a program needn't handle non-finite values.
Results may differ from a plain program's by a relative error of at most 0.0095.
Values may be sent and summed in bfloat16 or wider, within the bound.
A program may use at most 64 MiB of HBM per device.

v0:
```python
import jax
import jax.numpy as jnp
from jax import lax
from jax.sharding import PartitionSpec as P


def per_device(
    mode_shapes,
    amplitudes,
    self_resistance,
    out_factor,
    in_factor,
    block_source,
    block_cluster,
    block_rank,
):
    clusters, piece_rows, mode_count = mode_shapes.shape
    load_count = amplitudes.shape[1]
    blocks_per = out_factor.shape[1]
    rank_width = out_factor.shape[3]
    wide_count = lax.axis_size("wide")
    narrow_count = lax.axis_size("narrow")
    per_wide = clusters * blocks_per
    owner_index = lax.axis_index("wide")
    velocity = jnp.einsum(
        "cpm,ml->clp", mode_shapes, amplitudes, preferred_element_type=jnp.float32
    ).astype(jnp.bfloat16)
    near_load = (self_resistance[:, None, :] * velocity.astype(jnp.float32)).astype(jnp.bfloat16)
    source_table = block_source.reshape(wide_count, per_wide)
    cluster_table = block_cluster.reshape(wide_count, per_wide)
    rank_table = block_rank.reshape(wide_count, per_wide)
    my_source = lax.dynamic_index_in_dim(source_table, owner_index, 0, keepdims=False)
    my_cluster = lax.dynamic_index_in_dim(cluster_table, owner_index, 0, keepdims=False)
    my_rank = lax.dynamic_index_in_dim(rank_table, owner_index, 0, keepdims=False)
    gathered = lax.all_gather(velocity, "wide", axis=0, tiled=True)
    take_index = my_source * clusters + my_cluster
    pieces = jnp.take(gathered, take_index, axis=0)
    rights = in_factor.reshape(per_wide, piece_rows, rank_width)
    partial_value = jnp.einsum("blp,bpr->blr", pieces, rights, preferred_element_type=jnp.float32)
    summed = lax.psum(partial_value.astype(jnp.bfloat16), "narrow").astype(jnp.float32)
    rank_mask = (lax.iota(jnp.int32, rank_width)[None, :] < my_rank[:, None]).astype(jnp.float32)
    coeffs = (summed * rank_mask[:, None, :]).astype(jnp.bfloat16)
    left_blocks = out_factor.reshape(per_wide, piece_rows, rank_width)
    far_blocks = jnp.einsum("blr,bpr->blp", coeffs, left_blocks, preferred_element_type=jnp.float32)
    far_load = (
        far_blocks.reshape(clusters, blocks_per, load_count, piece_rows)
        .sum(axis=1)
        .astype(jnp.bfloat16)
    )
    patch_force = (near_load.astype(jnp.float32) + far_load.astype(jnp.float32)).astype(
        jnp.bfloat16
    )
    power_scale = (mode_count / (wide_count * narrow_count * clusters * piece_rows)) ** 0.5
    modal_load = lax.psum_scatter(
        jnp.einsum("cpm,clp->ml", mode_shapes, patch_force, preferred_element_type=jnp.float32)
        * power_scale,
        ("wide", "narrow"),
        scatter_dimension=0,
        tiled=True,
    )
    return (patch_force, modal_load)


def solution(mesh):
    return jax.shard_map(
        per_device,
        mesh=mesh,
        in_specs=(
            P(("groups", "wide"), "narrow", None),
            P("groups", "sub"),
            P(("groups", "wide"), "narrow"),
            P(("groups", "wide"), None, "narrow", None),
            P(("groups", "wide"), None, "narrow", None),
            P("groups", None),
            P("groups"),
            P("groups"),
        ),
        out_specs=(P(("groups", "wide"), "sub", "narrow"), P(("groups", "wide", "narrow"), "sub")),
        check_vma=False,
    )
```

profile of v0, /device:TPU:0, one launch (start us, length us, event | category | flops | bytes accessed | tf_op | source)
XLA Modules:
  0.0 144.6 jit_solution(15102335258527478778)
XLA Ops:
  7.2 0.0 copy-start
  7.2 0.0 all-reduce.2.cloned.1.call-start
  7.2 0.5 broadcast.68
  7.7 1.6 %reduce.3 = s32[48]{0:T(128)S(1)} reduce(s32[48,1]{0,1:T(1,128)} %param.13, s32[]{:T(128)} %broadcast.68), dimensions={1}, to_apply=%param.13.reduce_sub_computation.3 | reduce | bytes 388 | tf_op args[5]
  9.3 0.1 reshape.88
  9.4 0.7 reshape.89
  10.2 4.8 %fusion = bf16[6,32,512]{2,1,0:T(8,128)(2,1)S(1)} fusion(bf16[6,512,1024]{2,1,0:T(8,128)(2,1)} %param.8, bf16[1024,32]{0,1:T(8,128)(2,1)} %param.9), kind=kOutput, calls=%fused_computation.3 | convolution fusion | flops 201424896 | bytes 6553600 | tf_op jit(solution)/shard_map/cpm,ml->clp/dot_general | solution.py:25
  15.0 0.0 copy-start.3
  15.0 21.7 %all_gather.3 = bf16[24,32,512]{2,1,0:T(8,128)(2,1)} all-gather(bf16[6,32,512]{2,1,0:T(8,128)(2,1)S(1)} %fusion), channel_id=1, replica_groups=mesh['groups'=2,'wide'=4,'narrow'=2,'sub'=2] {'wide'}, dimensions={0}, use_global_device_ids=true | all-gather | bytes 983040 | tf_op jit(solution)/shard_map/all_gather | solution.py:35
  36.7 2.5 %gather_fusion = bf16[12,32,512]{2,1,0:T(8,128)(2,1)} fusion(bf16[24,32,512]{2,1,0:T(8,128)(2,1)} %all_gather.3, s32[1024]{0:T(1024)S(1)} %pad_clamp_fusion), kind=kCustom, calls=%fused_computation | custom fusion | bytes 786480 | tf_op jit(solution)/shard_map/jit(_take)/gather | solution.py:37
  39.2 3.4 %convolution_convert_fusion.1 = bf16[12,32,256]{2,1,0:T(8,128)(2,1)} fusion(bf16[12,512,256]{2,1,0:T(8,128)(2,1)} %bitcast.31, bf16[12,32,512]{2,1,0:T(8,128)(2,1)} %gather_fusion, pred[12]{0:T(512)(128)(4,1)S(1)} %get-tuple-element.2), kind=kOutput, calls=%fused_computation.2 | convolution fusion | flops 100958208 | bytes 3735564 | tf_op jit(solution)/shard_map/blp,bpr->blr/dot_general | solution.py:39
  42.6 0.0 copy-start.2
  42.6 0.0 all-reduce.2.cloned.1.call-update
  42.6 0.0 reduce-scatter.2.cloned.1.call-start
  42.6 0.0 copy-done.3
  42.6 0.1 reshape.91
  42.7 0.1 fusion.9
  42.8 22.0 %all-reduce.2.cloned.1.call-done = bf16[12,32,256]{2,1,0:T(8,128)(2,1)} async-done(((bf16[12,32,256]{2,1,0:T(8,128)(2,1)}), bf16[12,32,256]{2,1,0:T(8,128)(2,1)}) %all-reduce.2.cloned.1.call-update) | async-done | bytes 196624 | tf_op jit(solution)/shard_map/psum | solution.py:40
  64.8 0.0 copy-done
  64.8 2.8 %fusion.5 = f32[12,32,512]{2,1,0:T(8,128)} fusion(bf16[12,512,256]{2,1,0:T(8,128)(2,1)S(1)} %bitcast.30, bf16[12,32,256]{2,1,0:T(8,128)(2,1)} %all-reduce.2.cloned.1.call-done, f32[12,256]{1,0:T(8,128)S(1)} %fusion.9), kind=kOutput, calls=%fused_computation.12 | convolution fusion | flops 100958208 | bytes 4141056 | tf_op jit(solution)/shard_map/blr,bpr->blp/dot_general | solution.py:44
  67.6 1.9 %reduce_sum.9 = bf16[6,32,512]{2,1,0:T(8,128)(2,1)} reduce(f32[6,2,32,512]{3,2,1,0:T(8,128)} %bitcast.32, f32[]{:T(128)} %constant.34.clone.1), dimensions={1}, to_apply=%region_1.2 | reduce | flops 98304 | bytes 983044 | tf_op jit(solution)/shard_map/reduce_sum | solution.py:47
  69.6 0.0 copy-done.2
  69.6 1.0 add_convert_fusion
  70.5 0.0 copy-start.1
  70.6 4.7 %fusion.2 = f32[1024,32]{0,1:T(8,128)} fusion(bf16[6,32,512]{2,1,0:T(8,128)(2,1)S(1)} %add_convert_fusion, bf16[6,512,1024]{2,1,0:T(8,128)(2,1)} %param.8), kind=kOutput, calls=%fused_computation.6 | convolution fusion | flops 201359360 | bytes 6619136 | tf_op jit(solution)/shard_map/cpm,clp->ml/dot_general | solution.py:55
  75.2 0.0 copy-done.1
  75.2 0.0 reduce-scatter.2.cloned.1.call-update
  75.3 62.5 %reduce-scatter.2.cloned.1.call-done = f32[128,32]{0,1:T(8,128)} async-done(((f32[1024,32]{0,1:T(8,128)}), f32[128,32]{0,1:T(8,128)}) %reduce-scatter.2.cloned.1.call-update) | async-done | bytes 16400 | tf_op jit(solution)/shard_map/reduce_scatter | solution.py:54
  (4 shorter events, 0.0 us)
Async XLA Ops:
  7.2 57.6 %copy-start = (bf16[6,2,512,256]{3,2,1,0:T(8,128)(2,1)S(1)}, bf16[6,2,512,256]{3,2,1,0:T(8,128)(2,1)}, u32[]{:S(2)}) copy-start(bf16[6,2,512,256]{3,2,1,0:T(8,128)(2,1)} %param.11) | copy-start | bytes 9437188
  7.2 57.6 %all-reduce.2.cloned.1.call-start = ((), (), s32[]{:S(2)}) async-start(), calls=%async_computation.1 | async-start | bytes 393216 | tf_op jit(solution)/shard_map/psum | solution.py:40
  15.0 27.7 %copy-start.3 = (s32[48]{0:T(128)S(1)}, s32[48]{0:T(128)}, u32[]{:S(2)}) copy-start(s32[48]{0:T(128)} %param.15) | copy-start | bytes 580
  42.6 27.0 %copy-start.2 = (f32[6,512]{1,0:T(8,128)S(1)}, f32[6,512]{1,0:T(8,128)}, u32[]{:S(2)}) copy-start(f32[6,512]{1,0:T(8,128)} %param.10) | copy-start | bytes 36868
  42.6 95.2 %reduce-scatter.2.cloned.1.call-start = ((), (), s32[]{:S(2)}) async-start(), calls=%async_computation.2 | async-start | bytes 147456 | tf_op jit(solution)/shard_map/reduce_scatter | solution.py:54
  70.5 4.7 %copy-start.1 = (bf16[6,32,512]{2,1,0:T(8,128)(2,1)}, bf16[6,32,512]{2,1,0:T(8,128)(2,1)S(1)}, u32[]{:S(2)}) copy-start(bf16[6,32,512]{2,1,0:T(8,128)(2,1)S(1)} %add_convert_fusion) | copy-start | bytes 589828
Sparse Core Ops, SparseCore 0:
  42.7 22.0 all-reduce.1
  75.4 62.3 reduce-scatter.1
where the time goes:
time: 145 us
  waiting for transfers between devices  84.5 us (58%)
  blocking collectives  21.7 us (15%)
  matrix products  15.7 us (11%)
  between operations  14.1 us (10%)
  other arithmetic  4.6 us (3%)
  local copies, waits for them, and re-layouts  3.92 us (3%)
    reduce_scatter x1, waiting for transfers between devices, per_device(): lax.psum_scatter(jnp.einsum('cpm,clp->ml', mode_shapes, patch_force, pref...  62.5 us
    psum x1, waiting for transfers between devices, per_device(): lax.psum(partial_value.astype(jnp.bfloat16), 'narrow').astype(jnp.float32)  22 us
    all_gather x1, blocking collectives, per_device(): gathered = lax.all_gather(velocity, 'wide', axis=0, tiled=True)  21.7 us
    dot_general x1, matrix products, per_device(): jnp.einsum('cpm,ml->clp', mode_shapes, amplitudes, preferred_element_type...  4.76 us
    dot_general x1, matrix products, per_device(): jnp.einsum('cpm,clp->ml', mode_shapes, patch_force, preferred_element_typ...  4.68 us
    dot_general x1, matrix products, per_device(): jnp.einsum('blp,bpr->blr', pieces, rights, preferred_element_type=jnp.flo...  3.38 us
  transfers between devices with their start and end apart: 2, of which 2 were waited for; matrix products, arithmetic and copies ran while one was open for 0% of the time, Pallas kernels for 0%

commit v1 on v0

v1 whole, which is shorter than its diff:
```python
import functools

import jax
import jax.numpy as jnp
from jax import lax
from jax.experimental import pallas as pl
from jax.experimental.pallas import tpu as pltpu
from jax.sharding import PartitionSpec as P

MESH = pl.DeviceIdType.MESH
NT = (((1,), (1,)), ((), ()))


def partner(position, step, count):
    result, bit = 0, 1
    while bit < count:
        digit = lax.rem(lax.div(position, bit), 2)
        result = result + bit * ((1 - digit) if step & bit else digit)
        bit *= 2
    return result


def slots_of(source_ref, start, per_wide, wanted, cap):
    count = jnp.int32(0)
    rows = [jnp.int32(0)] * cap
    matches, counts = [], []
    for row in range(per_wide):
        hit = source_ref[start + row] == wanted
        for slot in range(cap):
            rows[slot] = jnp.where(hit & (count == slot), row, rows[slot])
        matches.append(hit)
        counts.append(jnp.minimum(count, cap - 1))
        count = count + jnp.where(hit, 1, 0)
    return rows, matches, counts


def kernel(
    wide_count, narrow_count, cap, split, dense, scale,
    source_ref, cluster_ref, rank_ref, amp_ref, res_ref, mode_hbm, in_hbm, out_hbm,
    force_hbm, modal_ref,
    mode_v, in_v, out_v, vel, near, force, outgoing, incoming, part_own, part_send, part_recv,
    coeffs, load_send, load_own, load_recv,
    mode_sem, in_sem, out_sem, force_sem, vel_send_sem, vel_recv_sem, part_send_sem, part_recv_sem,
    load_send_sem, load_recv_sem,
):
    wide, narrow = lax.axis_index("wide"), lax.axis_index("narrow")
    clusters, piece_rows, modes = mode_v.shape
    per_wide = in_v.shape[0]
    loads = vel.shape[1]
    rank_width = in_v.shape[2]
    group = cap // split

    mode_copies = [
        pltpu.make_async_copy(mode_hbm.at[c], mode_v.at[c], mode_sem.at[c]) for c in range(clusters)
    ]
    for copy in mode_copies:
        copy.start()
    in_copy = pltpu.make_async_copy(in_hbm, in_v, in_sem)
    in_copy.start()
    out_copy = pltpu.make_async_copy(out_hbm, out_v, out_sem)
    out_copy.start()

    wides = [partner(wide, step, wide_count) for step in range(wide_count)]
    narrows = [partner(narrow, step, narrow_count) for step in range(narrow_count)]
    barrier = pltpu.get_barrier_semaphore()
    for dw in range(wide_count):
        for dn in range(narrow_count):
            if dw or dn:
                pl.semaphore_signal(
                    barrier, inc=1, device_id={"wide": wides[dw], "narrow": narrows[dn]}, device_id_type=MESH
                )

    amps = amp_ref[...]
    own_start = wide * per_wide
    block_rows, slot_table = [], [jnp.int32(0)] * per_wide
    for dw in range(wide_count):
        rows, matches, counts = slots_of(source_ref, own_start, per_wide, wides[dw], cap)
        block_rows.append(rows)
        for row in range(per_wide):
            slot_table[row] = jnp.where(matches[row], dw * cap + counts[row], slot_table[row])
    wanted = []
    for dw in range(wide_count):
        rows, _, _ = slots_of(source_ref, wides[dw] * per_wide, per_wide, wide, cap)
        wanted.append([cluster_ref[wides[dw] * per_wide + row] for row in rows])

    for c in range(clusters):
        mode_copies[c].wait()
        vel[c] = lax.dot_general(amps, mode_v[c], NT, preferred_element_type=jnp.float32).astype(jnp.bfloat16)

    pl.semaphore_wait(barrier, wide_count * narrow_count - 1)

    def vel_copy(dw, slot):
        return pltpu.make_async_remote_copy(
            src_ref=outgoing.at[dw, slot],
            dst_ref=incoming.at[dw, slot],
            send_sem=vel_send_sem.at[dw, slot],
            recv_sem=vel_recv_sem.at[dw, slot],
            device_id={"wide": wides[dw]},
            device_id_type=MESH,
        )

    def part_copy(dw, piece, dn):
        span = pl.ds(piece * group, group)
        return pltpu.make_async_remote_copy(
            src_ref=part_send.at[dw, span],
            dst_ref=part_recv.at[dn, dw, span],
            send_sem=part_send_sem.at[dn, dw, piece],
            recv_sem=part_recv_sem.at[dn, dw, piece],
            device_id={"narrow": narrows[dn]},
            device_id_type=MESH,
        )

    def load_copy(dw, dn):
        return pltpu.make_async_remote_copy(
            src_ref=load_send.at[dw, narrows[dn]],
            dst_ref=load_recv.at[dw, dn],
            send_sem=load_send_sem.at[dw, dn],
            recv_sem=load_recv_sem.at[dw, dn],
            device_id={"wide": wides[dw], "narrow": narrows[dn]},
            device_id_type=MESH,
        )

    for dw in range(1, wide_count):
        for slot in range(cap):
            outgoing[dw, slot] = vel[wanted[dw][slot]]
            vel_copy(dw, slot).start()

    in_copy.wait()
    for dw in range(wide_count):
        for piece in range(split):
            for slot in range(piece * group, (piece + 1) * group):
                if dw:
                    vel_copy(dw, slot).wait_recv()
                    value = incoming[dw, slot]
                else:
                    value = vel[wanted[0][slot]]
                product = jnp.dot(value, in_v[block_rows[dw][slot]], preferred_element_type=jnp.float32)
                part_own[dw, slot] = product
                part_send[dw, slot] = product.astype(jnp.bfloat16)
            for dn in range(1, narrow_count):
                part_copy(dw, piece, dn).start()
        if dw == 0:
            for c in range(clusters):
                near[c] = (res_ref[pl.ds(c, 1), :] * vel[c].astype(jnp.float32)).astype(jnp.bfloat16)

    lanes = lax.broadcasted_iota(jnp.int32, (loads, rank_width), 1)
    for dw in range(wide_count):
        for piece in range(split):
            for dn in range(1, narrow_count):
                part_copy(dw, piece, dn).wait_recv()
            for slot in range(piece * group, (piece + 1) * group):
                total = part_own[dw, slot]
                for dn in range(1, narrow_count):
                    total = total + part_recv[dn, dw, slot].astype(jnp.float32)
                rank = rank_ref[own_start + block_rows[dw][slot]]
                coeffs[dw * cap + slot] = jnp.where(lanes < rank, total, 0.0).astype(jnp.bfloat16)

    out_copy.wait()
    blocks_per = per_wide // clusters
    for c in range(clusters):
        far = jnp.zeros((loads, piece_rows), jnp.float32)
        for k in range(blocks_per):
            row = c * blocks_per + k
            far = far + lax.dot_general(
                coeffs[slot_table[row]], out_v[row], NT, preferred_element_type=jnp.float32
            )
        far = far.astype(jnp.bfloat16).astype(jnp.float32)
        force[c] = (near[c].astype(jnp.float32) + far).astype(jnp.bfloat16)
    force_copy = pltpu.make_async_copy(force, force_hbm, force_sem)
    force_copy.start()

    order = list(range(1, wide_count))[::-1] + [0]
    if dense:
        columns = modes // wide_count
        rows = columns // narrow_count
        for dw in order:
            span = pl.ds(pl.multiple_of(wides[dw] * columns, 128), columns)
            total = jnp.zeros((loads, columns), jnp.float32)
            for c in range(clusters):
                total = total + jnp.dot(force[c], mode_v[c, :, span], preferred_element_type=jnp.float32)
            total = total * scale
            for n in range(narrow_count):
                piece = total[:, n * rows : (n + 1) * rows]
                load_send[dw, n] = piece.astype(load_send.dtype)
                if dw == 0:
                    load_own[n] = piece
            for dn in range(narrow_count):
                if dw or dn:
                    load_copy(dw, dn).start()
        result = load_own[narrow]
    else:
        total = jnp.zeros((loads, modes), jnp.float32)
        for c in range(clusters):
            total = total + jnp.dot(force[c], mode_v[c], preferred_element_type=jnp.float32)
        rows = modes // (wide_count * narrow_count)
        total = (total * scale).T.reshape(wide_count, narrow_count, rows, loads)
        for w in range(wide_count):
            load_own[w] = total[w]
        for dw in order:
            load_send[dw] = load_own[wides[dw]]
            for dn in range(narrow_count):
                if dw or dn:
                    load_copy(dw, dn).start()
        result = load_own[wide, narrow]
    for dw in order:
        for dn in range(narrow_count):
            if dw or dn:
                load_copy(dw, dn).wait_recv()
                result = result + load_recv[dw, dn].astype(jnp.float32)
    modal_ref[...] = result if dense else result.T

    force_copy.wait()
    for dw in range(wide_count):
        if dw:
            for slot in range(cap):
                vel_copy(dw, slot).wait_send()
        for dn in range(narrow_count):
            if dn:
                for piece in range(split):
                    part_copy(dw, piece, dn).wait_send()
            if dw or dn:
                load_copy(dw, dn).wait_send()


def per_device(
    mode_shapes,
    amplitudes,
    self_resistance,
    out_factor,
    in_factor,
    block_source,
    block_cluster,
    block_rank,
):
    clusters, piece_rows, modes = mode_shapes.shape
    loads = amplitudes.shape[1]
    blocks_per, rank_width = out_factor.shape[1], out_factor.shape[3]
    wide_count = lax.axis_size("wide")
    narrow_count = lax.axis_size("narrow")
    per_wide = clusters * blocks_per
    cap = min(per_wide, max(2, -(-per_wide // wide_count)))
    split = cap if wide_count <= 4 else 1
    rows = modes // (wide_count * narrow_count)
    dense = rows % 128 == 0
    scale = (modes / (wide_count * narrow_count * clusters * piece_rows)) ** 0.5
    bf16, f32 = jnp.bfloat16, jnp.float32
    if dense:
        load_shapes = [
            pltpu.VMEM((wide_count, narrow_count, loads, rows), bf16),
            pltpu.VMEM((narrow_count, loads, rows), f32),
            pltpu.VMEM((wide_count, narrow_count, loads, rows), bf16),
        ]
    else:
        load_shapes = [pltpu.VMEM((wide_count, narrow_count, rows, loads), f32)] * 3
    smem = pl.BlockSpec(memory_space=pltpu.SMEM)
    vmem = pl.BlockSpec(memory_space=pltpu.VMEM)
    hbm = pl.BlockSpec(memory_space=pl.ANY)
    dma = pltpu.SemaphoreType.DMA
    force, modal = pl.pallas_call(
        functools.partial(kernel, wide_count, narrow_count, cap, split, dense, scale),
        out_shape=(
            jax.ShapeDtypeStruct((clusters, loads, piece_rows), bf16),
            jax.ShapeDtypeStruct((loads, rows), f32),
        ),
        in_specs=[smem, smem, smem, vmem, vmem, hbm, hbm, hbm],
        out_specs=(hbm, vmem),
        scratch_shapes=[
            pltpu.VMEM((clusters, piece_rows, modes), bf16),
            pltpu.VMEM((per_wide, piece_rows, rank_width), bf16),
            pltpu.VMEM((per_wide, piece_rows, rank_width), bf16),
            pltpu.VMEM((clusters, loads, piece_rows), bf16),
            pltpu.VMEM((clusters, loads, piece_rows), bf16),
            pltpu.VMEM((clusters, loads, piece_rows), bf16),
            pltpu.VMEM((wide_count, cap, loads, piece_rows), bf16),
            pltpu.VMEM((wide_count, cap, loads, piece_rows), bf16),
            pltpu.VMEM((wide_count, cap, loads, rank_width), f32),
            pltpu.VMEM((wide_count, cap, loads, rank_width), bf16),
            pltpu.VMEM((narrow_count, wide_count, cap, loads, rank_width), bf16),
            pltpu.VMEM((wide_count * cap, loads, rank_width), bf16),
            *load_shapes,
            dma((clusters,)),
            dma,
            dma,
            dma,
            dma((wide_count, cap)),
            dma((wide_count, cap)),
            dma((narrow_count, wide_count, split)),
            dma((narrow_count, wide_count, split)),
            dma((wide_count, narrow_count)),
            dma((wide_count, narrow_count)),
        ],
        compiler_params=pltpu.CompilerParams(
            collective_id=0, has_side_effects=True, vmem_limit_bytes=60 * 1024 * 1024
        ),
    )(
        block_source.reshape(-1),
        block_cluster,
        block_rank,
        amplitudes.T,
        self_resistance,
        mode_shapes,
        in_factor.reshape(per_wide, piece_rows, rank_width),
        out_factor.reshape(per_wide, piece_rows, rank_width),
    )
    return force, modal.T


def solution(mesh):
    return jax.shard_map(
        per_device,
        mesh=mesh,
        in_specs=(
            P(("groups", "wide"), "narrow", None),
            P("groups", "sub"),
            P(("groups", "wide"), "narrow"),
            P(("groups", "wide"), None, "narrow", None),
            P(("groups", "wide"), None, "narrow", None),
            P("groups", None),
            P("groups"),
            P("groups"),
        ),
        out_specs=(P(("groups", "wide"), "sub", "narrow"), P(("groups", "wide", "narrow"), "sub")),
        check_vma=False,
    )
```

time: 145 us -> 31.4 us (0.22)
  waiting for transfers between devices: 84.5 us -> 0 us
  Pallas kernels: 0 us -> 27.5 us
  blocking collectives: 21.7 us -> 0 us
  matrix products: 15.7 us -> 0 us
  between operations: 14.1 us -> 0.64 us
  other arithmetic: 4.6 us -> 0 us
    reduce_scatter x1 -> x0, waiting for transfers between devices: 62.5 us -> none  [per_device(): lax.psum_scatter(jnp.einsum('cpm,clp->ml', mode_shapes, patch_force, pref...]
    pallas_call x0 -> x1, Pallas kernels: none -> 27.5 us  [per_device(): pl.pallas_call(functools.partial(kernel, wide_count, narrow_count, cap, s...]
    psum x1 -> x0, waiting for transfers between devices: 22 us -> none  [per_device(): lax.psum(partial_value.astype(jnp.bfloat16), 'narrow').astype(jnp.float32)]
    all_gather x1 -> x0, blocking collectives: 21.7 us -> none  [per_device(): gathered = lax.all_gather(velocity, 'wide', axis=0, tiled=True)]
    dot_general x4 -> x0, matrix products: 15.7 us -> none  [the longest x1 4.76 us: per_device(): jnp.einsum('cpm,ml->clp', mode_shapes, amplitudes, preferred_element_type...]
    gather x1 -> x0, local copies, waits for them, and re-layouts: 2.46 us -> none  [per_device(): pieces = jnp.take(gathered, take_index, axis=0)]
    unnamed x9 -> x2, local copies, waits for them, and re-layouts: 0.55 us -> 2.94 us
    reduce_sum x1 -> x0, other arithmetic: 1.92 us -> none  [per_device(): far_load = far_blocks.reshape(clusters, blocks_per, load_count, piece_row...]
  transfers between devices with their start and end apart: 2 -> 0, of which waited for: 2 -> 0; matrix products, arithmetic and copies ran while one was open for 0% -> 0% of each run, Pallas kernels for 0% -> 0%
where the time goes in v1:
time: 31.4 us; the launch traced here: 31.1 us
  Pallas kernels  27.5 us (88%)
  local copies, waits for them, and re-layouts  2.94 us (9%)
  between operations  0.64 us (2%)
    pallas_call x1, Pallas kernels, per_device(): pl.pallas_call(functools.partial(kernel, wide_count, narrow_count, cap, s...  27.5 us
    unnamed x2, local copies, waits for them, and re-layouts  2.94 us

profile of v1, /device:TPU:0, one launch (start us, length us, event | category | flops | bytes accessed | tf_op | source)
XLA Modules:
  0.0 31.1 jit_solution(8051937504622732261)
XLA Ops:
  0.6 27.5 %shard_map.95 = (bf16[6,32,512]{2,1,0:T(8,128)(2,1)}, f32[32,128]{1,0:T(8,128)}) custom-call(s32[48]{0:T(128)} %bitcast.9, s32[48]{0:T(128)} %cluster_ref.1, s32[48]{0:T(128)} %rank_ref.1, bf16[32,1024]{1,0:T(8,128)(2,1)} %bitcast.7, f32[6,512]{1,0:T(8,128)} %res_ref.1, bf16[6,512,1024]{2,1,0:T(8,128)(2,1)} %mode_hbm.1, bf16[12,512,256]{2,1,0:T(8,128)(2,1)} %bitcast.5, ...), custom_call_target="tpu_custom_call" | custom-call | tf_op jit(solution)/shard_map/pallas_call | solution.py:259
  28.2 1.6 %copy.12 = bf16[6,32,512]{2,1,0:T(8,128)(2,1)} copy(bf16[6,32,512]{2,1,0:T(8,128)(2,1)} %get-tuple-element.8) | data formatting | bytes 393216
  29.8 1.3 %copy.13 = f32[128,32]{0,1:T(8,128)} copy(f32[128,32]{0,1:T(8,128)} %bitcast.8) | data formatting | bytes 32768

commit v2 on v1

--- a/solution.py
+++ b/solution.py
@@ -36,11 +36,11 @@
 
 def kernel(
     wide_count, narrow_count, cap, split, dense, scale,
-    source_ref, cluster_ref, rank_ref, amp_ref, res_ref, mode_hbm, in_hbm, out_hbm,
-    force_hbm, modal_ref,
-    mode_v, in_v, out_v, vel, near, force, outgoing, incoming, part_own, part_send, part_recv,
+    source_hbm, cluster_hbm, rank_hbm, amp_hbm, res_hbm, mode_hbm, in_hbm, out_hbm,
+    force, modal_ref,
+    source_ref, cluster_ref, rank_ref, amp_ref, res_ref, mode_v, in_v, out_v, vel, near, outgoing, incoming, part_own, part_send, part_recv,
     coeffs, load_send, load_own, load_recv,
-    mode_sem, in_sem, out_sem, force_sem, vel_send_sem, vel_recv_sem, part_send_sem, part_recv_sem,
+    table_sem, mode_sem, in_sem, out_sem, vel_send_sem, vel_recv_sem, part_send_sem, part_recv_sem,
     load_send_sem, load_recv_sem,
 ):
     wide, narrow = lax.axis_index("wide"), lax.axis_index("narrow")
@@ -50,27 +50,44 @@
     rank_width = in_v.shape[2]
     group = cap // split
 
+    wides = [partner(wide, step, wide_count) for step in range(wide_count)]
+    narrows = [partner(narrow, step, narrow_count) for step in range(narrow_count)]
+    barrier = pltpu.get_barrier_semaphore()
+    for dw in range(wide_count):
+        for dn in range(narrow_count):
+            if dw or dn:
+                pl.semaphore_signal(
+                    barrier, inc=1, device_id={"wide": wides[dw], "narrow": narrows[dn]}, device_id_type=MESH
+                )
+
+    small_copies = [
+        pltpu.make_async_copy(src, dst, table_sem.at[i])
+        for i, (src, dst) in enumerate(
+            (
+                (source_hbm, source_ref),
+                (cluster_hbm, cluster_ref),
+                (amp_hbm, amp_ref),
+                (rank_hbm, rank_ref),
+                (res_hbm, res_ref),
+            )
+        )
+    ]
+    for copy in small_copies[:3]:
+        copy.start()
     mode_copies = [
         pltpu.make_async_copy(mode_hbm.at[c], mode_v.at[c], mode_sem.at[c]) for c in range(clusters)
     ]
     for copy in mode_copies:
         copy.start()
+    for copy in small_copies[3:]:
+        copy.start()
     in_copy = pltpu.make_async_copy(in_hbm, in_v, in_sem)
     in_copy.start()
     out_copy = pltpu.make_async_copy(out_hbm, out_v, out_sem)
     out_copy.start()
 
-    wides = [partner(wide, step, wide_count) for step in range(wide_count)]
-    narrows = [partner(narrow, step, narrow_count) for step in range(narrow_count)]
-    barrier = pltpu.get_barrier_semaphore()
-    for dw in range(wide_count):
-        for dn in range(narrow_count):
-            if dw or dn:
-                pl.semaphore_signal(
-                    barrier, inc=1, device_id={"wide": wides[dw], "narrow": narrows[dn]}, device_id_type=MESH
-                )
-
-    amps = amp_ref[...]
+    small_copies[0].wait()
+    small_copies[1].wait()
     own_start = wide * per_wide
     block_rows, slot_table = [], [jnp.int32(0)] * per_wide
     for dw in range(wide_count):
@@ -83,6 +100,8 @@
         rows, _, _ = slots_of(source_ref, wides[dw] * per_wide, per_wide, wide, cap)
         wanted.append([cluster_ref[wides[dw] * per_wide + row] for row in rows])
 
+    small_copies[2].wait()
+    amps = amp_ref[...]
     for c in range(clusters):
         mode_copies[c].wait()
         vel[c] = lax.dot_general(amps, mode_v[c], NT, preferred_element_type=jnp.float32).astype(jnp.bfloat16)
@@ -125,6 +144,8 @@
             outgoing[dw, slot] = vel[wanted[dw][slot]]
             vel_copy(dw, slot).start()
 
+    for copy in small_copies[3:]:
+        copy.wait()
     in_copy.wait()
     for dw in range(wide_count):
         for piece in range(split):
@@ -166,8 +187,6 @@
             )
         far = far.astype(jnp.bfloat16).astype(jnp.float32)
         force[c] = (near[c].astype(jnp.float32) + far).astype(jnp.bfloat16)
-    force_copy = pltpu.make_async_copy(force, force_hbm, force_sem)
-    force_copy.start()
 
     order = list(range(1, wide_count))[::-1] + [0]
     if dense:
@@ -209,7 +228,6 @@
                 result = result + load_recv[dw, dn].astype(jnp.float32)
     modal_ref[...] = result if dense else result.T
 
-    force_copy.wait()
     for dw in range(wide_count):
         if dw:
             for slot in range(cap):
@@ -220,6 +238,11 @@
                     part_copy(dw, piece, dn).wait_send()
             if dw or dn:
                 load_copy(dw, dn).wait_send()
+
+
+def finish(force_ref, modal_ref, force_out, modal_out):
+    force_out[...] = force_ref[...]
+    modal_out[...] = modal_ref[...]
 
 
 def per_device(
@@ -252,7 +275,6 @@
         ]
     else:
         load_shapes = [pltpu.VMEM((wide_count, narrow_count, rows, loads), f32)] * 3
-    smem = pl.BlockSpec(memory_space=pltpu.SMEM)
     vmem = pl.BlockSpec(memory_space=pltpu.VMEM)
     hbm = pl.BlockSpec(memory_space=pl.ANY)
     dma = pltpu.SemaphoreType.DMA
@@ -262,13 +284,17 @@
             jax.ShapeDtypeStruct((clusters, loads, piece_rows), bf16),
             jax.ShapeDtypeStruct((loads, rows), f32),
         ),
-        in_specs=[smem, smem, smem, vmem, vmem, hbm, hbm, hbm],
-        out_specs=(hbm, vmem),
+        in_specs=[hbm] * 8,
+        out_specs=(vmem, vmem),
         scratch_shapes=[
+            pltpu.SMEM(block_cluster.shape, jnp.int32),
+            pltpu.SMEM(block_cluster.shape, jnp.int32),
+            pltpu.SMEM(block_cluster.shape, jnp.int32),
+            pltpu.VMEM((loads, modes), bf16),
+            pltpu.VMEM((clusters, piece_rows), f32),
             pltpu.VMEM((clusters, piece_rows, modes), bf16),
             pltpu.VMEM((per_wide, piece_rows, rank_width), bf16),
             pltpu.VMEM((per_wide, piece_rows, rank_width), bf16),
-            pltpu.VMEM((clusters, loads, piece_rows), bf16),
             pltpu.VMEM((clusters, loads, piece_rows), bf16),
             pltpu.VMEM((clusters, loads, piece_rows), bf16),
             pltpu.VMEM((wide_count, cap, loads, piece_rows), bf16),
@@ -278,8 +304,8 @@
             pltpu.VMEM((narrow_count, wide_count, cap, loads, rank_width), bf16),
             pltpu.VMEM((wide_count * cap, loads, rank_width), bf16),
             *load_shapes,
+            dma((5,)),
             dma((clusters,)),
-            dma,
             dma,
             dma,
             dma((wide_count, cap)),
@@ -302,6 +328,15 @@
         in_factor.reshape(per_wide, piece_rows, rank_width),
         out_factor.reshape(per_wide, piece_rows, rank_width),
     )
+    force, modal = pl.pallas_call(
+        finish,
+        out_shape=(
+            jax.ShapeDtypeStruct(force.shape, bf16),
+            jax.ShapeDtypeStruct(modal.shape, f32),
+        ),
+        in_specs=[vmem] * 2,
+        out_specs=(vmem, vmem),
+    )(force, modal)
     return force, modal.T
 
 

time: 31.4 us -> 29.8 us (0.949)
  local copies, waits for them, and re-layouts: 2.94 us -> 0 us
  Pallas kernels: 27.5 us -> 29.1 us
    unnamed x2 -> x0, local copies, waits for them, and re-layouts: 2.94 us -> none
    pallas_call x0 -> x1, Pallas kernels: none -> 1.62 us  [per_device(): pl.pallas_call(finish, out_shape=(jax.ShapeDtypeStruct(force.shape, bf16)...]
where the time goes in v2:
time: 29.8 us; the launch traced here: 29.7 us
  Pallas kernels  29.1 us (98%)
  between operations  0.64 us (2%)
    pallas_call x1, Pallas kernels, per_device(): pl.pallas_call(functools.partial(kernel, wide_count, narrow_count, cap, s...  27.4 us
    pallas_call x1, Pallas kernels, per_device(): pl.pallas_call(finish, out_shape=(jax.ShapeDtypeStruct(force.shape, bf16)...  1.62 us

profile of v2, /device:TPU:0, one launch (start us, length us, event | category | flops | bytes accessed | tf_op | source)
XLA Modules:
  0.0 29.7 jit_solution(15408604397448510305)
XLA Ops:
  0.6 27.4 %shard_map.95 = (bf16[6,32,512]{2,1,0:T(8,128)(2,1)}, f32[32,128]{1,0:T(8,128)}) custom-call(s32[48]{0:T(128)} %bitcast.8, s32[48]{0:T(128)} %cluster_hbm.1, s32[48]{0:T(128)} %rank_hbm.1, bf16[32,1024]{1,0:T(8,128)(2,1)} %bitcast.7, f32[6,512]{1,0:T(8,128)} %res_hbm.1, bf16[6,512,1024]{2,1,0:T(8,128)(2,1)} %mode_hbm.1, bf16[12,512,256]{2,1,0:T(8,128)(2,1)} %bitcast.5, ...), custom_call_target="tpu_custom_call" | custom-call | tf_op jit(solution)/shard_map/pallas_call | solution.py:281
  28.1 1.6 %shard_map.96 = (bf16[6,32,512]{2,1,0:T(8,128)(2,1)}, f32[32,128]{1,0:T(8,128)}) custom-call(bf16[6,32,512]{2,1,0:T(8,128)(2,1)} %get-tuple-element.6.force_ref, f32[32,128]{1,0:T(8,128)} %get-tuple-element.7.modal_ref), custom_call_target="tpu_custom_call" | custom-call | tf_op jit(solution)/shard_map/pallas_call | solution.py:331

commit v3 on v2

--- a/solution.py
+++ b/solution.py
@@ -316,9 +316,9 @@
             dma((wide_count, narrow_count)),
         ],
         compiler_params=pltpu.CompilerParams(
-            collective_id=0, has_side_effects=True, vmem_limit_bytes=60 * 1024 * 1024
+            collective_id=0, has_side_effects=True, vmem_limit_bytes=40 * 1024 * 1024
         ),
-    )(
+    )(*(pltpu.with_memory_space_constraint(operand, pltpu.HBM) for operand in (
         block_source.reshape(-1),
         block_cluster,
         block_rank,
@@ -327,7 +327,7 @@
         mode_shapes,
         in_factor.reshape(per_wide, piece_rows, rank_width),
         out_factor.reshape(per_wide, piece_rows, rank_width),
-    )
+    )))
     force, modal = pl.pallas_call(
         finish,
         out_shape=(
@@ -336,6 +336,7 @@
         ),
         in_specs=[vmem] * 2,
         out_specs=(vmem, vmem),
+        compiler_params=pltpu.CompilerParams(vmem_limit_bytes=4 * 1024 * 1024),
     )(force, modal)
     return force, modal.T
 

time: 29.8 us -> 28.2 us (0.946)
  Pallas kernels: 29.1 us -> 27.4 us
    pallas_call x1, Pallas kernels: 1.62 us -> 0.69 us  [per_device(): pl.pallas_call(finish, out_shape=(jax.ShapeDtypeStruct(force.shape, bf16)...]
    pallas_call x1, Pallas kernels: 27.4 us -> 26.8 us  [per_device(): pl.pallas_call(functools.partial(kernel, wide_count, narrow_count, cap, s...]
where the time goes in v3:
time: 28.2 us; the launch traced here: 28.1 us
  Pallas kernels  27.4 us (97%)
  between operations  0.64 us (2%)
    pallas_call x1, Pallas kernels, per_device(): pl.pallas_call(functools.partial(kernel, wide_count, narrow_count, cap, s...  26.8 us
    pallas_call x1, Pallas kernels, per_device(): pl.pallas_call(finish, out_shape=(jax.ShapeDtypeStruct(force.shape, bf16)...  0.69 us

profile of v3, /device:TPU:0, one launch (start us, length us, event | category | flops | bytes accessed | tf_op | source)
XLA Modules:
  0.0 28.1 jit_solution(13159926870662594418)
XLA Ops:
  0.6 26.8 %shard_map.95 = (bf16[6,32,512]{2,1,0:T(8,128)(2,1)S(1)}, f32[32,128]{1,0:T(8,128)S(1)}) custom-call(s32[48]{0:T(128)} %bitcast.8, s32[48]{0:T(128)} %cluster_hbm.1, s32[48]{0:T(128)} %rank_hbm.1, bf16[32,1024]{1,0:T(8,128)(2,1)} %bitcast.7, f32[6,512]{1,0:T(8,128)} %res_hbm.1, bf16[6,512,1024]{2,1,0:T(8,128)(2,1)} %mode_hbm.1, ...), custom_call_target="tpu_custom_call" | custom-call | tf_op jit(solution)/shard_map/pallas_call | solution.py:281
  27.4 0.7 %shard_map.96 = (bf16[6,32,512]{2,1,0:T(8,128)(2,1)}, f32[32,128]{1,0:T(8,128)}) custom-call(bf16[6,32,512]{2,1,0:T(8,128)(2,1)S(1)} %get-tuple-element.6.force_ref, f32[32,128]{1,0:T(8,128)S(1)} %get-tuple-element.7.modal_ref), custom_call_target="tpu_custom_call" | custom-call | tf_op jit(solution)/shard_map/pallas_call | solution.py:331
